TPU v7x, 32 devices: a whole 2x2x4 slice. The times are simulated.
32 devices in a mesh: space: 16 (over z, x, core), trial: 2 (over y).
Axes of the slice: x: 2, y: 2, z: 4, core: 2. Of those that a mesh axis runs over, the one named last changes fastest.
Arguments:
- trial_x: bfloat16 [4, 4096, 1024], P('trial', 'space')
- h_panel: bfloat16 [4096, 640], P('space')
- s_panel: bfloat16 [4096, 640], P('space')
- pattern: int32 [64, 10], P('space'), may hold values from 0 to 63, as said below
Outputs:
- theta: float32 [4], P('trial')
- new_dirs: bfloat16 [4, 4096, 1024], P('trial', 'space')
- mean_sq: float32 [4], P('trial')
Inputs may be any that keep to these rules, and one draw needn't show every extreme that they name: pattern[a, 0] is a; the entries of a row are distinct atoms of a's own spatial domain or of the two domains beside it (cyclically), the domain of atom a being a // 4.
All inputs are finite; a program needn't handle non-finite values.
Results may differ from a plain program's by a relative error of at most 0.0006.
Values may be sent and summed in bfloat16 or wider, within the bound.
A program may use at most 128 MiB of HBM per device.

v0:
```python
import jax
import jax.numpy as jnp
from jax import lax
from jax.sharding import PartitionSpec as P


def padded(x, sides, width):
    for axis, dim in sides:
        peers, length = (lax.axis_size(axis), x.shape[dim])
        up = [(i, (i + 1) % peers) for i in range(peers)]
        down = [(j, i) for i, j in up]
        last = lax.slice_in_dim(x, length - width, length, axis=dim)
        first = lax.slice_in_dim(x, 0, width, axis=dim)
        before = lax.ppermute(last, axis, up)
        after = lax.ppermute(first, axis, down)
        x = jnp.concatenate([before, x, after], axis=dim)
    return x


def neighbours(values, width):
    return padded(values, (("space", 1),), width)


def apply_tiles(h_panel, s_panel, links, extended, block):
    count, ext_rows, width = extended.shape
    atom_dev, slots = links.shape
    blocks = extended.reshape(count, ext_rows // block, block, width)
    picked = blocks[:, links]
    h_tiles = h_panel.reshape(atom_dev, block, slots, block)
    s_tiles = s_panel.reshape(atom_dev, block, slots, block)
    h_image = jnp.einsum("apbq,kabqw->kapw", h_tiles, picked, preferred_element_type=jnp.float32)
    s_image = jnp.einsum("apbq,kabqw->kapw", s_tiles, picked, preferred_element_type=jnp.float32)
    return (h_image.reshape(count, -1), s_image.reshape(count, -1))


def row_reduce(section, values):
    if section == "ritz":
        return lax.psum(values, "space")
    if section == "project":
        return lax.psum(values, "space")
    return lax.psum(values, "space")


def solve_coeffs(gram, correlation):
    factor = jnp.linalg.cholesky(gram)
    return jax.scipy.linalg.cho_solve((factor, True), correlation)


def finish(x_every, mine_shape, flat_h, flat_s, reducer, total):
    flat_all = x_every.reshape(x_every.shape[0], -1)
    gram_part = jnp.dot(flat_all, flat_all.T, preferred_element_type=jnp.float32)
    wide_all = flat_all.astype(jnp.float32)
    cross = jnp.sum(flat_s * flat_h, axis=1)
    weight = jnp.sum(flat_s * flat_s, axis=1)
    cross, weight, gram = reducer("ritz", (cross, weight, gram_part))
    theta = cross / (weight + 1e-06)
    flat_r = flat_h - theta[:, None] * flat_s
    correlation = reducer("project", jnp.dot(wide_all, flat_r.T, precision=lax.Precision.HIGHEST))
    coeffs = solve_coeffs(gram, correlation)
    normal_part = flat_r - jnp.dot(coeffs.T, wide_all, precision=lax.Precision.HIGHEST)
    mean_sq = reducer("norm", jnp.sum(normal_part * normal_part, axis=1)) / total
    scaled = normal_part * lax.rsqrt(mean_sq + 1e-06)[:, None]
    return (theta, scaled.astype(jnp.bfloat16).reshape(mine_shape), mean_sq)


def on_device(trial_x, h_panel, s_panel, pattern):
    atom_dev = pattern.shape[0]
    block = h_panel.shape[0] // atom_dev
    domains = lax.axis_size("space")
    atoms = atom_dev * domains
    links = jnp.mod(pattern - lax.axis_index("space") * atom_dev + atom_dev, atoms)
    total = float(atoms * block * trial_x.shape[2])
    x_every = lax.all_gather(trial_x, "trial", axis=0, tiled=True)
    flat_h, flat_s = apply_tiles(
        h_panel, s_panel, links, neighbours(trial_x, atom_dev * block), block
    )
    theta, normed, mean_sq = finish(x_every, trial_x.shape, flat_h, flat_s, row_reduce, total)
    return (theta, normed, mean_sq)


def solution(mesh):
    in_specs = (P("trial", "space", None), P("space", None), P("space", None), P("space", None))
    out_specs = (P("trial"), P("trial", "space", None), P("trial"))
    return jax.shard_map(
        on_device, mesh=mesh, in_specs=in_specs, out_specs=out_specs, check_vma=False
    )
```

profile of v0, /device:TPU:0, one launch (start us, length us, event | category | flops | bytes accessed | tf_op | source)
XLA Modules:
  0.0 193.7 jit_solution(5035406191406211222)
XLA Ops:
  7.2 0.0 copy-start.8
  7.2 0.0 all-gather.2.cloned.1.call-start
  7.2 0.5 collective-permute-start
  7.7 5.0 %collective-permute-start.1 = (bf16[2,256,1024]{2,1,0:T(8,128)(2,1)}, bf16[2,256,1024]{2,1,0:T(8,128)(2,1)}, u32[]{:S(2)}, u32[]{:S(2)}) collective-permute-start(bf16[2,256,1024]{2,1,0:T(8,128)(2,1)} %param.4), channel_id=1, source_target_pairs={{2,0},{4,2},{6,4},{8,6},{10,8},{12,10},{14,12},{16,14},{18,16},{20... | collective-permute-start | bytes 3145736 | tf_op jit(solution)/shard_map/ppermute | solution.py:15
  12.8 0.0 all-gather.2.cloned.1.call-update
  12.8 0.7 compare_select_fusion
  13.5 0.1 reshape.56
  13.6 2.4 %reshape.70 = bf16[4,64,10,64]{3,2,1,0:T(8,128)(2,1)} reshape(bf16[256,640]{1,0:T(8,128)(2,1)} %param.5) | data formatting | bytes 655360 | tf_op jit(solution)/shard_map/reshape | solution.py:29
  16.0 0.0 copy-done.8
  16.0 1.6 reshape.69
  17.6 7.9 %collective-permute-done = bf16[2,256,1024]{2,1,0:T(8,128)(2,1)S(1)} collective-permute-done((bf16[2,256,1024]{2,1,0:T(8,128)(2,1)}, bf16[2,256,1024]{2,1,0:T(8,128)(2,1)S(1)}, u32[]{:S(2)}, u32[]{:S(2)}) %collective-permute-start) | collective-permute-done | bytes 1048608 | tf_op jit(solution)/shard_map/ppermute | solution.py:14
  25.5 0.0 copy-start.7
  25.5 1.0 copy-done.7
  26.5 0.0 collective-permute-done.1
  26.5 2.0 %pad_maximum_fusion = bf16[2,768,1024]{2,1,0:T(8,128)(2,1)S(1)} fusion(bf16[2,256,1024]{2,1,0:T(8,128)(2,1)} %collective-permute-done.1, bf16[2,256,1024]{2,1,0:T(8,128)(2,1)} %param.4, bf16[2,256,1024]{2,1,0:T(8,128)(2,1)} %copy-done.7), kind=kLoop, calls=%fused_computation.6 | loop fusion | flops 9437184 | bytes 6291456 | tf_op jit(solution)/shard_map/concatenate | solution.py:16
  28.5 5.8 %gather_fusion = bf16[40,2,64,1024]{3,2,1,0:T(8,128)(2,1)} fusion(bf16[2,12,64,1024]{3,2,1,0:T(8,128)(2,1)S(1)} %bitcast.54, s32[1024]{0:T(1024)S(1)} %pad_clamp_fusion), kind=kCustom, calls=%fused_computation | custom fusion | bytes 20971680 | tf_op jit(solution)/shard_map/gather | solution.py:28
  34.2 0.0 copy-start
  34.2 0.0 copy-start.6
  34.2 6.5 %fusion.6 = f32[2,4,64,1024]{3,2,0,1:T(8,128)S(1)} fusion(bf16[2,4,10,64,1024]{4,3,0,2,1:T(8,128)(2,1)} %bitcast.55, bf16[4,64,10,64,1]{3,2,1,0,4:T(8,128)(2,1)} %bitcast.68), kind=kOutput, calls=%fused_computation.14 | convolution fusion | flops 671088640 | bytes 12910592 | tf_op jit(solution)/shard_map/apbq,kabqw->kapw/dot_general | solution.py:31
  40.7 0.8 copy-done
  41.5 0.2 copy-done.6
  41.7 3.5 %multiply_reduce_fusion.1 = (f32[2]{0:T(128)S(1)}, f32[2]{0:T(128)S(1)}, f32[2,4,64,1024]{3,2,0,1:T(8,128)}) fusion(f32[2,4,64,1024]{3,2,0,1:T(8,128)S(1)} %fusion.6, bf16[2,4,10,64,1024]{4,3,0,2,1:T(8,128)(2,1)S(1)} %bitcast.56, bf16[4,64,10,64,1]{3,2,1,0,4:T(8,128)(2,1)S(1)} %bitcast.67), kind=kOutput, calls=%fused_computation.10 | convolution fusion | flops 673185792 | bytes 15007760 | tf_op jit(solution)/shard_map/apbq,kabqw->kapw/dot_general | solution.py:32
  45.2 39.6 %all-reduce.1 = (f32[2]{0:T(128)S(1)}, f32[2]{0:T(128)S(1)}) all-reduce(f32[2]{0:T(128)S(1)} %get-tuple-element.4, f32[2]{0:T(128)S(1)} %get-tuple-element.3), channel_id=1, replica_groups=mesh['space'=16,'trial'=2] {'space'}, use_global_device_ids=true, to_apply=%region_1.2 | all-reduce | flops 4 | bytes 32 | tf_op jit(solution)/shard_map/psum | solution.py:38
  84.8 0.0 copy-start.1
  84.8 1.4 copy.32
  86.2 0.9 copy-done.1
  87.2 0.1 copy.33
  87.3 0.0 copy-start.9
  87.3 0.5 multiply_subtract_fusion
  87.8 0.1 copy.39
  88.0 2.9 %copy.56 = f32[1,2,256,1024]{3,1,2,0:T(2,128)} copy(f32[1,2,256,1024]{3,2,1,0:T(8,128)S(1)} %bitcast.59) | data formatting | bytes 4194304
  90.9 1.6 copy.55
  92.5 0.0 all-gather.2.cloned.1.call-done
  92.6 0.0 copy-start.5
  92.6 3.4 %copy.57 = bf16[1,4,256,1024]{3,1,2,0:T(4,128)(2,1)S(1)} copy(bf16[1,4,256,1024]{3,2,1,0:T(8,128)(2,1)} %bitcast.61) | data formatting | bytes 4194304
  95.9 0.0 copy-start.4
  95.9 1.3 copy-done.4
  97.3 0.0 copy-done.5
  97.3 0.0 copy-start.3
  97.3 9.2 %convolution_bitcast_fusion = f32[4,2]{0,1:T(2,128)S(1)} fusion(f32[2,262144]{1,0:T(2,128)S(1)} %bitcast.66, bf16[4,262144]{1,0:T(4,128)(2,1)S(1)} %bitcast.63), kind=kOutput, calls=%fused_computation.17 | convolution fusion | flops 25165824 | bytes 4194336 | tf_op jit(solution)/shard_map/dot_general | solution.py:58
  106.4 0.0 copy-done.3
  106.4 0.0 copy-start.2
  106.4 3.5 %fusion.12 = f32[4,4]{0,1:T(4,128)S(1)} fusion(bf16[4,256,1024]{2,1,0:T(8,128)(2,1)S(1)} %copy-done.3), kind=kOutput, calls=%fused_computation.16 | convolution fusion | flops 8388608 | bytes 2097216 | tf_op jit(solution)/shard_map/dot_general | solution.py:51
  110.0 0.0 copy-done.2
  110.0 2.9 %copy.54 = f32[1,2,256,1024]{3,1,2,0:T(2,128)} copy(f32[1,2,256,1024]{3,2,1,0:T(8,128)S(1)} %bitcast.57) | data formatting | bytes 4194304
  112.9 29.5 %all-reduce = (f32[4,2]{0,1:T(2,128)S(1)}, f32[4,4]{0,1:T(4,128)S(1)}) all-reduce(f32[4,2]{0,1:T(2,128)S(1)} %convolution_bitcast_fusion, f32[4,4]{0,1:T(4,128)S(1)} %fusion.12), channel_id=1, replica_groups=mesh['space'=16,'trial'=2] {'space'}, use_global_device_ids=true, to_apply=%region_7.8 | all-reduce | flops 24 | bytes 192 | tf_op jit(solution)/shard_map/psum | solution.py:40
  142.4 0.1 copy.37
  142.5 0.4 cholesky.16
  142.9 0.6 compare_reduce_fusion
  143.5 0.6 fusion.17
  144.2 0.3 custom-call.10
  144.5 0.1 fusion.19
  144.6 0.1 fusion.21
  144.8 0.0 copy-done.9
  144.8 8.7 %multiply_reduce_fusion = (f32[2]{0:T(128)S(1)}, f32[2,262144]{1,0:T(2,128)}) fusion(f32[4,2]{0,1:T(2,128)S(1)} %fusion.21, bf16[4,262144]{1,0:T(4,128)(2,1)} %bitcast.64, f32[2,262144]{1,0:T(2,128)} %bitcast.65, f32[2,262144]{1,0:T(2,128)S(1)} %bitcast.62, f32[2]{0:T(128)S(1)} %add_divide_fusion), kind=kOutput, calls=%fused_computation.8 | convolution fusion | flops 27787262 | bytes 8388656 | tf_op jit(solution)/shard_map/dot_general | solution.py:60
  153.5 29.5 %psum.39 = f32[2]{0:T(128)S(1)} all-reduce(f32[2]{0:T(128)S(1)} %get-tuple-element.12), channel_id=1, replica_groups=mesh['space'=16,'trial'=2] {'space'}, use_global_device_ids=true, to_apply=%region_9.10 | all-reduce | flops 2 | bytes 16 | tf_op jit(solution)/shard_map/psum | solution.py:41
  183.0 0.5 add_rsqrt_fusion
  183.5 2.1 %multiply_convert_fusion = bf16[2,262144]{1,0:T(2,128)(2,1)S(1)} fusion(f32[2,262144]{1,0:T(2,128)} %get-tuple-element.13, f32[2]{0:T(128)S(1)} %get-tuple-element.9), kind=kLoop, calls=%fused_computation.7 | loop fusion | flops 1048576 | bytes 3145736 | tf_op jit(solution)/shard_map/convert_element_type | solution.py:63
  185.6 1.2 copy.80
  (4 shorter events, 0.0 us)
Async XLA Ops:
  7.2 8.8 %copy-start.8 = (bf16[256,640]{1,0:T(8,128)(2,1)S(1)}, bf16[256,640]{1,0:T(8,128)(2,1)}, u32[]{:S(2)}) copy-start(bf16[256,640]{1,0:T(8,128)(2,1)} %param.6) | copy-start | bytes 983044
  7.2 85.4 %all-gather.2.cloned.1.call-start = ((), (), s32[]{:S(2)}) async-start(), calls=%async_computation | async-start | bytes 3145728 | tf_op jit(solution)/shard_map/all_gather | solution.py:73
  7.2 18.3 %collective-permute-start = (bf16[2,256,1024]{2,1,0:T(8,128)(2,1)}, bf16[2,256,1024]{2,1,0:T(8,128)(2,1)S(1)}, u32[]{:S(2)}, u32[]{:S(2)}) collective-permute-start(bf16[2,256,1024]{2,1,0:T(8,128)(2,1)} %param.4), channel_id=1, source_target_pairs={{0,2},{2,4},{4,6},{6,8},{8,10},{10,12},{12,14},{14,16},{16,18},{18... | collective-permute-start | bytes 3145736 | tf_op jit(solution)/shard_map/ppermute | solution.py:14
  7.7 18.7 %collective-permute-start.1 = (bf16[2,256,1024]{2,1,0:T(8,128)(2,1)}, bf16[2,256,1024]{2,1,0:T(8,128)(2,1)}, u32[]{:S(2)}, u32[]{:S(2)}) collective-permute-start(bf16[2,256,1024]{2,1,0:T(8,128)(2,1)} %param.4), channel_id=1, source_target_pairs={{2,0},{4,2},{6,4},{8,6},{10,8},{12,10},{14,12},{16,14},{18,16},{20... | collective-permute-start | bytes 3145736 | tf_op jit(solution)/shard_map/ppermute | solution.py:15
  25.5 1.0 copy-start.7
  34.2 7.3 %copy-start = (bf16[40,2,64,1024]{3,2,1,0:T(8,128)(2,1)S(1)}, bf16[40,2,64,1024]{3,2,1,0:T(8,128)(2,1)}, u32[]{:S(2)}) copy-start(bf16[40,2,64,1024]{3,2,1,0:T(8,128)(2,1)} %gather_fusion) | copy-start | bytes 31457284
  34.2 7.5 %copy-start.6 = (bf16[4,64,10,64]{3,2,1,0:T(8,128)(2,1)S(1)}, bf16[4,64,10,64]{3,2,1,0:T(8,128)(2,1)}, u32[]{:S(2)}) copy-start(bf16[4,64,10,64]{3,2,1,0:T(8,128)(2,1)} %reshape.69) | copy-start | bytes 983044
  84.8 2.3 %copy-start.1 = (f32[2,4,64,1024]{3,2,0,1:T(8,128)S(1)}, f32[2,4,64,1024]{3,2,0,1:T(8,128)}, u32[]{:S(2)}) copy-start(f32[2,4,64,1024]{3,2,0,1:T(8,128)} %get-tuple-element.11) | copy-start | bytes 6291460
  87.3 57.5 %copy-start.9 = (f32[2]{0:T(128)}, f32[2]{0:T(128)S(1)}, u32[]{:S(2)}) copy-start(f32[2]{0:T(128)S(1)} %add_divide_fusion) | copy-start | bytes 28
  92.6 4.7 %copy-start.5 = (f32[1,2,256,1024]{3,1,2,0:T(2,128)S(1)}, f32[1,2,256,1024]{3,1,2,0:T(2,128)}, u32[]{:S(2)}) copy-start(f32[1,2,256,1024]{3,1,2,0:T(2,128)} %copy.56) | copy-start | bytes 6291460
  95.9 1.4 copy-start.4
  97.3 9.2 %copy-start.3 = (bf16[4,256,1024]{2,1,0:T(8,128)(2,1)S(1)}, bf16[4,256,1024]{2,1,0:T(8,128)(2,1)}, u32[]{:S(2)}) copy-start(bf16[4,256,1024]{2,1,0:T(8,128)(2,1)} %all-gather.2.cloned.1.call-done) | copy-start | bytes 6291460
  106.4 3.5 %copy-start.2 = (f32[2,4,64,1024]{3,2,1,0:T(8,128)S(1)}, f32[2,4,64,1024]{3,2,1,0:T(8,128)}, u32[]{:S(2)}) copy-start(f32[2,4,64,1024]{3,2,1,0:T(8,128)} %copy.32) | copy-start | bytes 6291460
Sparse Core Ops, SparseCore 0:
  12.9 32.4 all-gather.1
where the time goes:
time: 194 us
  blocking collectives  98.5 us (51%)
  matrix products  31.6 us (16%)
  local copies, waits for them, and re-layouts  28 us (14%)
  between operations  14.2 us (7%)
  waiting for transfers between devices  7.97 us (4%)
  other arithmetic  7.8 us (4%)
  starting transfers between devices  5.57 us (3%)
    psum x3, blocking collectives, row_reduce(): return lax.psum(values, 'space')  98.5 us
    unnamed x25, local copies, waits for them, and re-layouts  16.4 us
    dot_general x1, matrix products, finish(): jnp.dot(wide_all, flat_r.T, precision=lax.Precision.HIGHEST)  9.15 us
    dot_general x1, matrix products, finish(): jnp.dot(coeffs.T, wide_all, precision=lax.Precision.HIGHEST)  8.71 us
    ppermute x1, waiting for transfers between devices, padded(): before = lax.ppermute(last, axis, up)  7.93 us
    dot_general x1, matrix products, apply_tiles(): jnp.einsum('apbq,kabqw->kapw', h_tiles, picked, preferred_element_type=jn...  6.46 us
    gather x1, local copies, waits for them, and re-layouts, apply_tiles(): picked = blocks[:, links]  5.77 us
    ppermute x1, starting transfers between devices, padded(): after = lax.ppermute(first, axis, down)  5.03 us
  transfers between devices with their start and end apart: 3, of which 1 were waited for; matrix products, arithmetic and copies ran while one was open for 15% of the time, Pallas kernels for 0%

commit v1 on v0

v1 whole, which is shorter than its diff:
```python
import functools

import jax
import jax.numpy as jnp
from jax import lax
from jax.experimental import pallas as pl
from jax.experimental.pallas import tpu as pltpu
from jax.sharding import PartitionSpec as P

F32, BF16 = jnp.float32, jnp.bfloat16
GROUP = 30


def stat_pairs(own, states):
    pairs = [(("s", k), ("h", k)) for k in range(own)]
    pairs += [(("s", k), ("s", k)) for k in range(own)]
    pairs += [(("x", t), ("h", k)) for t in range(states) for k in range(own)]
    pairs += [(("x", t), ("s", k)) for t in range(states) for k in range(own)]
    pairs += [(("x", t), ("x", u)) for t in range(states) for u in range(t + 1)]
    return pairs


def cholesky_solve(gram, rhs):
    n = len(rhs)
    low = [[None] * n for _ in range(n)]
    inv = [None] * n
    for j in range(n):
        d = gram[j][j]
        for k in range(j):
            d = d - low[j][k] * low[j][k]
        inv[j] = 1.0 / jnp.sqrt(d)
        for i in range(j + 1, n):
            v = gram[i][j]
            for k in range(j):
                v = v - low[i][k] * low[j][k]
            low[i][j] = v * inv[j]
    out = []
    for col in range(len(rhs[0])):
        y = []
        for i in range(n):
            v = rhs[i][col]
            for k in range(i):
                v = v - low[i][k] * y[k]
            y.append(v * inv[i])
        z = [None] * n
        for i in reversed(range(n)):
            v = y[i]
            for k in range(i + 1, n):
                v = v - low[k][i] * z[k]
            z[i] = v * inv[i]
        out.append(z)
    return out


def body(domains, groups, chunk, pat, x, h, s, out, theta_o, msq_o,
         ext, oth, hp, sp, pick, hext, img, acc, slots, nslots, obuf,
         lsem, osem, nb_send, nb_recv, tr_send, tr_recv, st_send, st_recv, nm_send, nm_recv):
    own, rows, width = x.shape
    atoms_dev, nslot = pat.shape
    block = rows // atoms_dev
    atoms = atoms_dev * domains
    span = 3 * rows
    states = own * groups
    chunks = width // chunk
    me, mt = lax.axis_index("space"), lax.axis_index("trial")
    right, left = lax.rem(me + 1, domains), lax.rem(me + domains - 1, domains)

    loads = [
        pltpu.make_async_copy(x, ext.at[:, pl.ds(rows, rows), :], lsem.at[0]),
        pltpu.make_async_copy(h, hp, lsem.at[1]),
        pltpu.make_async_copy(s, sp, lsem.at[2]),
    ]
    for load in loads:
        load.start()

    barrier = pltpu.get_barrier_semaphore()

    def greet(k, carry):
        pl.semaphore_signal(barrier, inc=1, device_id={"space": lax.rem(me + k, domains)})
        return carry
    lax.fori_loop(1, domains, greet, 0)
    for k in range(1, groups):
        pl.semaphore_signal(barrier, inc=1, device_id={"trial": lax.rem(mt + k, groups)})
    pl.semaphore_wait(barrier, domains - 1 + groups - 1)

    def neighbour_copy(side, c):
        cols = pl.ds(pl.multiple_of(c * chunk, chunk), chunk)
        return pltpu.make_async_remote_copy(
            src_ref=x.at[:, :, cols],
            dst_ref=ext.at[:, pl.ds(2 * rows * side, rows), cols],
            send_sem=nb_send.at[side, c], recv_sem=nb_recv.at[side, c],
            device_id={"space": left if side else right})

    def trial_copy(k, c):
        cols = pl.ds(pl.multiple_of(c * chunk, chunk), chunk)
        return pltpu.make_async_remote_copy(
            src_ref=x.at[:, :, cols], dst_ref=oth.at[k - 1, :, :, cols],
            send_sem=tr_send.at[k - 1, c], recv_sem=tr_recv.at[k - 1, c],
            device_id={"trial": lax.rem(mt + k, groups)})

    def arrivals(c):
        return [neighbour_copy(0, c), neighbour_copy(1, c)] + [trial_copy(k, c) for k in range(1, groups)]

    for c in range(chunks):
        for copy in arrivals(c):
            copy.start()

    acc[...] = jnp.zeros_like(acc)
    loads[1].wait()
    loads[2].wait()
    diff = (lax.broadcasted_iota(jnp.int32, (block, span), 1)
            - lax.broadcasted_iota(jnp.int32, (block, span), 0))

    def densify(a, carry):
        for b in range(nslot):
            link = lax.rem(pat[a, b] - me * atoms_dev + atoms_dev + atoms, atoms)
            pick[b * block:(b + 1) * block, :] = jnp.where(diff == link * block, 1.0, 0.0).astype(BF16)
        at = pl.multiple_of(a * block, block)
        ha = jnp.dot(hp[pl.ds(at, block), :], pick[...], preferred_element_type=F32)
        hext[pl.ds(at, block), :] = ha.astype(BF16)
        sa = jnp.dot(sp[pl.ds(at, block), :], pick[...], preferred_element_type=F32)
        hext[pl.ds(pl.multiple_of(rows + a * block, block), block), :] = sa.astype(BF16)
        return carry
    lax.fori_loop(0, atoms_dev, densify, 0)
    loads[0].wait()

    pairs = stat_pairs(own, states)

    def fetch(name, at, col):
        kind, k = name
        cols = pl.ds(pl.multiple_of(col, 128), 128)
        if kind == "h":
            return img[k, pl.ds(at, 16), cols]
        if kind == "s":
            return img[k, pl.ds(pl.multiple_of(rows + at, 16), 16), cols]
        if k < own:
            return ext[k, pl.ds(pl.multiple_of(rows + at, 16), 16), cols].astype(F32)
        return oth[k // own - 1, k % own, pl.ds(at, 16), cols].astype(F32)

    def on_chunk(c, carry):
        for copy in arrivals(c):
            copy.wait_recv()
        cols = pl.ds(pl.multiple_of(c * chunk, chunk), chunk)
        for k in range(own):
            img[k, :, cols] = jnp.dot(hext[...], ext[k, :, cols], preferred_element_type=F32)
        for first in range(0, len(pairs), GROUP):
            part = pairs[first:first + GROUP]

            def on_rows(r, sums):
                at = pl.multiple_of(r * 16, 16)
                for piece in range(chunk // 128):
                    have = {}
                    new = []
                    for (a, b), total in zip(part, sums):
                        for name in (a, b):
                            if name not in have:
                                have[name] = fetch(name, at, c * chunk + piece * 128)
                        p = have[a] * have[b]
                        new.append(total + (p[:8] + p[8:]))
                    sums = tuple(new)
                return sums
            zero = jnp.zeros((8, 128), F32)
            sums = lax.fori_loop(0, rows // 16, on_rows, (zero,) * len(part))
            for i, v in enumerate(sums):
                acc[first + i] += v
        return carry
    lax.fori_loop(0, chunks, on_chunk, 0)

    lane = lax.broadcasted_iota(jnp.int32, (8, 128), 1)
    message = jnp.zeros((8, 128), F32)
    for g in range(acc.shape[0] // 8):
        lines = jnp.sum(acc[g * 8:(g + 1) * 8], axis=1)
        ends = jnp.sum(lines, axis=1, keepdims=True)
        message = jnp.where(lane == g, jnp.broadcast_to(ends, (8, 128)), message)

    def share(buffer, send, recv):
        def copy(k):
            return pltpu.make_async_remote_copy(
                src_ref=buffer.at[me], dst_ref=buffer.at[me],
                send_sem=send.at[k], recv_sem=recv.at[me],
                device_id={"space": lax.rem(me + k, domains)})

        def go(k, carry):
            copy(k).start()
            return carry
        lax.fori_loop(1, domains, go, 0)

        def come(k, carry):
            peer = lax.rem(me + k, domains)
            pltpu.make_async_remote_copy(
                src_ref=buffer.at[peer], dst_ref=buffer.at[peer],
                send_sem=send.at[k], recv_sem=recv.at[peer],
                device_id={"space": peer}).wait_recv()
            return carry
        lax.fori_loop(1, domains, come, 0)

        def left_here(k, carry):
            copy(k).wait_send()
            return carry
        return lambda: lax.fori_loop(1, domains, left_here, 0)

    slots[me] = message
    end_stats = share(slots, st_send, st_recv)
    total = slots[0]
    for d in range(1, domains):
        total = total + slots[d]
    value = {}
    for i, name in enumerate(pairs):
        value[name] = jnp.broadcast_to(total[i % 8:i % 8 + 1, i // 8:i // 8 + 1], (8, 128))
    theta = [value[("s", k), ("h", k)] / (value[("s", k), ("s", k)] + 1e-06) for k in range(own)]
    corr = [[value[("x", t), ("h", k)] - theta[k] * value[("x", t), ("s", k)] for k in range(own)]
            for t in range(states)]
    gram = [[value[("x", t), ("x", u)] for u in range(t + 1)] for t in range(states)]
    coeffs = cholesky_solve(gram, corr)
    for k in range(own):
        theta_o[k] = theta[k][0, 0]

    def wide(v):
        return jnp.concatenate([v, v], axis=0)

    zero = jnp.zeros((8, 128), F32)

    def on_normal(r, sums):
        at = pl.multiple_of(r * 16, 16)
        sums = list(sums)
        for col in range(0, width, 128):
            xs = [fetch(("x", t), at, col) for t in range(states)]
            for k in range(own):
                n = fetch(("h", k), at, col) - wide(theta[k]) * fetch(("s", k), at, col)
                lump = wide(coeffs[k][0]) * xs[0]
                for t in range(1, states):
                    lump = lump + wide(coeffs[k][t]) * xs[t]
                n = n - lump
                img[k, pl.ds(at, 16), pl.ds(col, 128)] = n
                p = n * n
                sums[k] = sums[k] + (p[:8] + p[8:])
        return tuple(sums)
    sums = lax.fori_loop(0, rows // 16, on_normal, (zero,) * own)
    for k in range(own):
        nslots[me, k] = sums[k]
    end_norms = share(nslots, nm_send, nm_recv)
    scale = []
    for k in range(own):
        v = nslots[0, k]
        for d in range(1, domains):
            v = v + nslots[d, k]
        v = jnp.sum(jnp.sum(v, axis=0, keepdims=True), axis=1, keepdims=True)
        mean = jnp.broadcast_to(v, (8, 128)) / float(domains * rows * width)
        msq_o[k] = mean[0, 0]
        scale.append(wide(lax.rsqrt(mean + 1e-06)))
    stores = []
    for k in range(own):
        def on_scale(r, carry):
            at = pl.multiple_of(r * 16, 16)
            for col in range(0, width, 128):
                v = img[k, pl.ds(at, 16), pl.ds(col, 128)] * scale[k]
                obuf[k, pl.ds(at, 16), pl.ds(col, 128)] = v.astype(BF16)
            return carry
        lax.fori_loop(0, rows // 16, on_scale, 0)
        store = pltpu.make_async_copy(obuf.at[k], out.at[k], osem.at[k])
        store.start()
        stores.append(store)
    for c in range(chunks):
        for copy in arrivals(c):
            copy.wait_send()
    end_stats()
    end_norms()
    for store in stores:
        store.wait()


def on_device(domains, groups, trial_x, h_panel, s_panel, pattern):
    own, rows, width = trial_x.shape
    depth = h_panel.shape[1]
    chunk = 256
    chunks = width // chunk
    stats = -(-len(stat_pairs(own, own * groups)) // 8) * 8
    dma = pltpu.SemaphoreType.DMA
    new_dirs, theta, mean_sq = pl.pallas_call(
        functools.partial(body, domains, groups, chunk),
        out_shape=(jax.ShapeDtypeStruct(trial_x.shape, BF16),
                   jax.ShapeDtypeStruct((own,), F32), jax.ShapeDtypeStruct((own,), F32)),
        in_specs=[pl.BlockSpec(memory_space=pltpu.SMEM)] + [pl.BlockSpec(memory_space=pl.ANY)] * 3,
        out_specs=(pl.BlockSpec(memory_space=pl.ANY), pl.BlockSpec(memory_space=pltpu.SMEM),
                   pl.BlockSpec(memory_space=pltpu.SMEM)),
        scratch_shapes=[
            pltpu.VMEM((own, 3 * rows, width), BF16),
            pltpu.VMEM((groups - 1, own, rows, width), BF16),
            pltpu.VMEM((rows, depth), BF16),
            pltpu.VMEM((rows, depth), BF16),
            pltpu.VMEM((depth, 3 * rows), BF16),
            pltpu.VMEM((2 * rows, 3 * rows), BF16),
            pltpu.VMEM((own, 2 * rows, width), F32),
            pltpu.VMEM((stats, 8, 128), F32),
            pltpu.VMEM((domains, 8, 128), F32),
            pltpu.VMEM((domains, own, 8, 128), F32),
            pltpu.VMEM((own, rows, width), BF16),
            dma((3,)), dma((own,)),
            dma((2, chunks)), dma((2, chunks)),
            dma((groups - 1, chunks)), dma((groups - 1, chunks)),
            dma((domains,)), dma((domains,)), dma((domains,)), dma((domains,)),
        ],
        compiler_params=pltpu.CompilerParams(
            collective_id=0, has_side_effects=True, vmem_limit_bytes=40 * 1024 * 1024),
    )(pattern, trial_x, h_panel, s_panel)
    return theta, new_dirs, mean_sq


def solution(mesh):
    in_specs = (P("trial", "space", None), P("space", None), P("space", None), P("space", None))
    out_specs = (P("trial"), P("trial", "space", None), P("trial"))
    return jax.shard_map(
        functools.partial(on_device, mesh.shape["space"], mesh.shape["trial"]),
        mesh=mesh, in_specs=in_specs, out_specs=out_specs, check_vma=False
    )
```

time: 194 us -> 53 us (0.27)
  blocking collectives: 98.5 us -> 0 us
  Pallas kernels: 0 us -> 46.2 us
  matrix products: 31.6 us -> 0 us
  local copies, waits for them, and re-layouts: 28 us -> 5.84 us
  between operations: 14.2 us -> 0.65 us
  waiting for transfers between devices: 7.97 us -> 0 us
  other arithmetic: 7.8 us -> 0 us
  starting transfers between devices: 5.57 us -> 0 us
    psum x3 -> x0, blocking collectives: 98.5 us -> none  [row_reduce(): return lax.psum(values, 'space')]
    pallas_call x0 -> x1, Pallas kernels: none -> 46.2 us  [on_device(): pl.pallas_call(functools.partial(body, domains, groups, chunk), out_shape...]
    dot_general x5 -> x0, matrix products: 31.3 us -> none  [the longest x1 9.15 us: finish(): jnp.dot(wide_all, flat_r.T, precision=lax.Precision.HIGHEST)]
    unnamed x25 -> x11, local copies, waits for them, and re-layouts: 16.4 us -> 5.84 us
    ppermute x2 -> x0, waiting for transfers between devices: 7.93 us -> none  [the longest x1 7.93 us: padded(): before = lax.ppermute(last, axis, up)]
    gather x1 -> x0, local copies, waits for them, and re-layouts: 5.77 us -> none  [apply_tiles(): picked = blocks[:, links]]
    ppermute x2 -> x0, starting transfers between devices: 5.54 us -> none  [the longest x1 5.03 us: padded(): after = lax.ppermute(first, axis, down)]
    reshape x2 -> x0, local copies, waits for them, and re-layouts: 3.99 us -> none  [the longest x1 2.38 us: apply_tiles(): h_tiles = h_panel.reshape(atom_dev, block, slots, block)]
  transfers between devices with their start and end apart: 3 -> 0, of which waited for: 1 -> 0; matrix products, arithmetic and copies ran while one was open for 15% -> 0% of each run, Pallas kernels for 0% -> 0%
where the time goes in v1:
time: 53 us; the launch traced here: 52.7 us
  Pallas kernels  46.2 us (87%)
  local copies, waits for them, and re-layouts  5.84 us (11%)
  between operations  0.65 us (1%)
    pallas_call x1, Pallas kernels, on_device(): pl.pallas_call(functools.partial(body, domains, groups, chunk), out_shape...  46.2 us
    unnamed x11, local copies, waits for them, and re-layouts  5.84 us

profile of v1, /device:TPU:0, one launch (start us, length us, event | category | flops | bytes accessed | tf_op | source)
XLA Modules:
  0.0 52.7 jit_solution(7203292361925890174)
XLA Ops:
  0.6 0.0 copy-start
  0.6 1.2 %copy-done = bf16[2,256,1024]{2,1,0:T(8,128)(2,1)S(1)} copy-done((bf16[2,256,1024]{2,1,0:T(8,128)(2,1)S(1)}, bf16[2,256,1024]{2,1,0:T(8,128)(2,1)}, u32[]{:S(2)}) %copy-start) | copy-done | bytes 1048600
  1.9 0.0 copy-start.1
  1.9 1.0 %copy-done.1 = bf16[256,640]{1,0:T(8,128)(2,1)S(1)} copy-done((bf16[256,640]{1,0:T(8,128)(2,1)S(1)}, bf16[256,640]{1,0:T(8,128)(2,1)}, u32[]{:S(2)}) %copy-start.1) | copy-done | bytes 327704
  2.8 0.0 copy-start.2
  2.8 1.0 %copy-done.2 = bf16[256,640]{1,0:T(8,128)(2,1)S(1)} copy-done((bf16[256,640]{1,0:T(8,128)(2,1)S(1)}, bf16[256,640]{1,0:T(8,128)(2,1)}, u32[]{:S(2)}) %copy-start.2) | copy-done | bytes 327704
  3.8 0.0 copy-start.3
  3.8 0.7 %copy-done.3 = s32[4,10]{1,0:T(4,128)S(1)} copy-done((s32[4,10]{1,0:T(4,128)S(1)}, s32[4,10]{1,0:T(4,128)}, u32[]{:S(2)}) %copy-start.3) | copy-done | bytes 184
  4.5 46.2 %shard_map.67 = (bf16[2,256,1024]{2,1,0:T(8,128)(2,1)S(1)}, f32[2]{0:T(128)S(1)}, f32[2]{0:T(128)S(1)}) custom-call(s32[4,10]{1,0:T(4,128)S(1)} %copy-done.3, bf16[2,256,1024]{2,1,0:T(8,128)(2,1)S(1)} %copy-done, bf16[256,640]{1,0:T(8,128)(2,1)S(1)} %copy-done.1, bf16[256,640]{1,0:T(8,128)(2,1)S(1)} %copy-done.2), custom_call_target="tpu_custom_call" | custom-call | tf_op jit(solution)/shard_map/pallas_call | solution.py:279
  50.7 0.5 copy.10
  51.2 1.0 %copy.11 = bf16[2,256,1024]{2,1,0:T(8,128)(2,1)} copy(bf16[2,256,1024]{2,1,0:T(8,128)(2,1)S(1)} %get-tuple-element.13) | data formatting | bytes 2097152
  52.2 0.5 copy.12
Async XLA Ops:
  0.6 1.2 %copy-start = (bf16[2,256,1024]{2,1,0:T(8,128)(2,1)S(1)}, bf16[2,256,1024]{2,1,0:T(8,128)(2,1)}, u32[]{:S(2)}) copy-start(bf16[2,256,1024]{2,1,0:T(8,128)(2,1)} %x.1) | copy-start | bytes 3145732
  1.9 1.0 %copy-start.1 = (bf16[256,640]{1,0:T(8,128)(2,1)S(1)}, bf16[256,640]{1,0:T(8,128)(2,1)}, u32[]{:S(2)}) copy-start(bf16[256,640]{1,0:T(8,128)(2,1)} %h.1) | copy-start | bytes 983044
  2.8 1.0 %copy-start.2 = (bf16[256,640]{1,0:T(8,128)(2,1)S(1)}, bf16[256,640]{1,0:T(8,128)(2,1)}, u32[]{:S(2)}) copy-start(bf16[256,640]{1,0:T(8,128)(2,1)} %s.1) | copy-start | bytes 983044
  3.8 0.7 %copy-start.3 = (s32[4,10]{1,0:T(4,128)S(1)}, s32[4,10]{1,0:T(4,128)}, u32[]{:S(2)}) copy-start(s32[4,10]{1,0:T(4,128)} %pat.1) | copy-start | bytes 484

commit v2 on v1

--- a/solution.py
+++ b/solution.py
@@ -52,9 +52,9 @@
     return out
 
 
-def body(domains, groups, chunk, pat, x, h, s, out, theta_o, msq_o,
-         ext, oth, hp, sp, pick, hext, img, acc, slots, nslots, obuf,
-         lsem, osem, nb_send, nb_recv, tr_send, tr_recv, st_send, st_recv, nm_send, nm_recv):
+def body(domains, groups, chunk, pat_hbm, x, h, s, out, facts,
+         pat, ext, oth, hp, sp, pick, hext, img, acc, slots, nslots,
+         lsem, nb_send, nb_recv, tr_send, tr_recv, st_send, st_recv, nm_send, nm_recv):
     own, rows, width = x.shape
     atoms_dev, nslot = pat.shape
     block = rows // atoms_dev
@@ -69,6 +69,7 @@
         pltpu.make_async_copy(x, ext.at[:, pl.ds(rows, rows), :], lsem.at[0]),
         pltpu.make_async_copy(h, hp, lsem.at[1]),
         pltpu.make_async_copy(s, sp, lsem.at[2]),
+        pltpu.make_async_copy(pat_hbm, pat, lsem.at[3]),
     ]
     for load in loads:
         load.start()
@@ -108,6 +109,7 @@
     acc[...] = jnp.zeros_like(acc)
     loads[1].wait()
     loads[2].wait()
+    loads[3].wait()
     diff = (lax.broadcasted_iota(jnp.int32, (block, span), 1)
             - lax.broadcasted_iota(jnp.int32, (block, span), 0))
 
@@ -166,12 +168,15 @@
         return carry
     lax.fori_loop(0, chunks, on_chunk, 0)
 
-    lane = lax.broadcasted_iota(jnp.int32, (8, 128), 1)
-    message = jnp.zeros((8, 128), F32)
-    for g in range(acc.shape[0] // 8):
-        lines = jnp.sum(acc[g * 8:(g + 1) * 8], axis=1)
-        ends = jnp.sum(lines, axis=1, keepdims=True)
-        message = jnp.where(lane == g, jnp.broadcast_to(ends, (8, 128)), message)
+    lines = slots.shape[1]
+    spot = (lax.broadcasted_iota(jnp.int32, (8, 128), 1)
+            - lax.broadcasted_iota(jnp.int32, (8, 128), 0))
+    for line in range(lines):
+        message = jnp.zeros((8, 128), F32)
+        for g in range(16 * line, min(16 * line + 16, acc.shape[0] // 8)):
+            ends = jnp.sum(jnp.sum(acc[g * 8:(g + 1) * 8], axis=1), axis=1, keepdims=True)
+            message = jnp.where(spot == (g % 16) * 8, jnp.broadcast_to(ends, (8, 128)), message)
+        slots[me, line:line + 1] = jnp.sum(message, axis=0, keepdims=True)
 
     def share(buffer, send, recv):
         def copy(k):
@@ -199,21 +204,20 @@
             return carry
         return lambda: lax.fori_loop(1, domains, left_here, 0)
 
-    slots[me] = message
     end_stats = share(slots, st_send, st_recv)
     total = slots[0]
     for d in range(1, domains):
         total = total + slots[d]
     value = {}
     for i, name in enumerate(pairs):
-        value[name] = jnp.broadcast_to(total[i % 8:i % 8 + 1, i // 8:i // 8 + 1], (8, 128))
+        value[name] = jnp.broadcast_to(total[i // 128:i // 128 + 1, i % 128:i % 128 + 1], (8, 128))
     theta = [value[("s", k), ("h", k)] / (value[("s", k), ("s", k)] + 1e-06) for k in range(own)]
     corr = [[value[("x", t), ("h", k)] - theta[k] * value[("x", t), ("s", k)] for k in range(own)]
             for t in range(states)]
     gram = [[value[("x", t), ("x", u)] for u in range(t + 1)] for t in range(states)]
     coeffs = cholesky_solve(gram, corr)
     for k in range(own):
-        theta_o[k] = theta[k][0, 0]
+        facts[k] = theta[k][0, 0]
 
     def wide(v):
         return jnp.concatenate([v, v], axis=0)
@@ -231,42 +235,25 @@
                 for t in range(1, states):
                     lump = lump + wide(coeffs[k][t]) * xs[t]
                 n = n - lump
-                img[k, pl.ds(at, 16), pl.ds(col, 128)] = n
+                out[k, pl.ds(at, 16), pl.ds(col, 128)] = n
                 p = n * n
                 sums[k] = sums[k] + (p[:8] + p[8:])
         return tuple(sums)
     sums = lax.fori_loop(0, rows // 16, on_normal, (zero,) * own)
     for k in range(own):
-        nslots[me, k] = sums[k]
+        nslots[me, k:k + 1] = jnp.sum(sums[k], axis=0, keepdims=True)
     end_norms = share(nslots, nm_send, nm_recv)
-    scale = []
+    norm = nslots[0]
+    for d in range(1, domains):
+        norm = norm + nslots[d]
+    norm = jnp.sum(norm, axis=1, keepdims=True) / float(domains * rows * width)
     for k in range(own):
-        v = nslots[0, k]
-        for d in range(1, domains):
-            v = v + nslots[d, k]
-        v = jnp.sum(jnp.sum(v, axis=0, keepdims=True), axis=1, keepdims=True)
-        mean = jnp.broadcast_to(v, (8, 128)) / float(domains * rows * width)
-        msq_o[k] = mean[0, 0]
-        scale.append(wide(lax.rsqrt(mean + 1e-06)))
-    stores = []
-    for k in range(own):
-        def on_scale(r, carry):
-            at = pl.multiple_of(r * 16, 16)
-            for col in range(0, width, 128):
-                v = img[k, pl.ds(at, 16), pl.ds(col, 128)] * scale[k]
-                obuf[k, pl.ds(at, 16), pl.ds(col, 128)] = v.astype(BF16)
-            return carry
-        lax.fori_loop(0, rows // 16, on_scale, 0)
-        store = pltpu.make_async_copy(obuf.at[k], out.at[k], osem.at[k])
-        store.start()
-        stores.append(store)
+        facts[own + k] = norm[k, 0]
     for c in range(chunks):
         for copy in arrivals(c):
             copy.wait_send()
     end_stats()
     end_norms()
-    for store in stores:
-        store.wait()
 
 
 def on_device(domains, groups, trial_x, h_panel, s_panel, pattern):
@@ -276,14 +263,13 @@
     chunks = width // chunk
     stats = -(-len(stat_pairs(own, own * groups)) // 8) * 8
     dma = pltpu.SemaphoreType.DMA
-    new_dirs, theta, mean_sq = pl.pallas_call(
+    normal, facts = pl.pallas_call(
         functools.partial(body, domains, groups, chunk),
-        out_shape=(jax.ShapeDtypeStruct(trial_x.shape, BF16),
-                   jax.ShapeDtypeStruct((own,), F32), jax.ShapeDtypeStruct((own,), F32)),
-        in_specs=[pl.BlockSpec(memory_space=pltpu.SMEM)] + [pl.BlockSpec(memory_space=pl.ANY)] * 3,
-        out_specs=(pl.BlockSpec(memory_space=pl.ANY), pl.BlockSpec(memory_space=pltpu.SMEM),
-                   pl.BlockSpec(memory_space=pltpu.SMEM)),
+        out_shape=(jax.ShapeDtypeStruct(trial_x.shape, F32), jax.ShapeDtypeStruct((2 * own,), F32)),
+        in_specs=[pl.BlockSpec(memory_space=pltpu.HBM)] * 4,
+        out_specs=(pl.BlockSpec(memory_space=pltpu.VMEM), pl.BlockSpec(memory_space=pltpu.SMEM)),
         scratch_shapes=[
+            pltpu.SMEM(pattern.shape, jnp.int32),
             pltpu.VMEM((own, 3 * rows, width), BF16),
             pltpu.VMEM((groups - 1, own, rows, width), BF16),
             pltpu.VMEM((rows, depth), BF16),
@@ -292,18 +278,19 @@
             pltpu.VMEM((2 * rows, 3 * rows), BF16),
             pltpu.VMEM((own, 2 * rows, width), F32),
             pltpu.VMEM((stats, 8, 128), F32),
-            pltpu.VMEM((domains, 8, 128), F32),
-            pltpu.VMEM((domains, own, 8, 128), F32),
-            pltpu.VMEM((own, rows, width), BF16),
-            dma((3,)), dma((own,)),
+            pltpu.VMEM((domains, -(-stats // 128), 128), F32),
+            pltpu.VMEM((domains, own, 128), F32),
+            dma((4,)),
             dma((2, chunks)), dma((2, chunks)),
             dma((groups - 1, chunks)), dma((groups - 1, chunks)),
             dma((domains,)), dma((domains,)), dma((domains,)), dma((domains,)),
         ],
         compiler_params=pltpu.CompilerParams(
             collective_id=0, has_side_effects=True, vmem_limit_bytes=40 * 1024 * 1024),
-    )(pattern, trial_x, h_panel, s_panel)
-    return theta, new_dirs, mean_sq
+    )(*[pltpu.with_memory_space_constraint(v, pltpu.HBM) for v in (pattern, trial_x, h_panel, s_panel)])
+    theta, mean_sq = facts[:own], facts[own:]
+    scaled = normal * lax.rsqrt(mean_sq + 1e-06)[:, None, None]
+    return theta, scaled.astype(BF16), mean_sq
 
 
 def solution(mesh):

time: 53 us -> 46.4 us (0.88)
  local copies, waits for them, and re-layouts: 5.84 us -> 0 us
  Pallas kernels: 46.2 us -> 43.7 us
  other arithmetic: 0 us -> 1.85 us
    unnamed x11 -> x0, local copies, waits for them, and re-layouts: 5.84 us -> none
    pallas_call x1, Pallas kernels: 46.2 us -> 43.7 us  [on_device(): pl.pallas_call(functools.partial(body, domains, groups, chunk), out_shape...]
    convert_element_type x0 -> x1, other arithmetic: none -> 1.27 us  [on_device(): return (theta, scaled.astype(BF16), mean_sq)]
    rsqrt x0 -> x1, other arithmetic: none -> 0.58 us  [on_device(): scaled = normal * lax.rsqrt(mean_sq + 1e-06)[:, None, None]]
where the time goes in v2:
time: 46.4 us; the launch traced here: 46.2 us
  Pallas kernels  43.7 us (94%)
  other arithmetic  1.85 us (4%)
  between operations  0.64 us (1%)
    pallas_call x1, Pallas kernels, on_device(): pl.pallas_call(functools.partial(body, domains, groups, chunk), out_shape...  43.7 us
    convert_element_type x1, other arithmetic, on_device(): return (theta, scaled.astype(BF16), mean_sq)  1.27 us

profile of v2, /device:TPU:0, one launch (start us, length us, event | category | flops | bytes accessed | tf_op | source)
XLA Modules:
  0.0 46.2 jit_solution(16544149458633308732)
XLA Ops:
  0.6 43.7 %shard_map.67 = (f32[2,256,1024]{2,1,0:T(8,128)S(1)}, f32[4]{0:T(128)S(1)}) custom-call(s32[4,10]{1,0:T(4,128)} %pat_hbm.1, bf16[2,256,1024]{2,1,0:T(8,128)(2,1)} %x.1, bf16[256,640]{1,0:T(8,128)(2,1)} %h.1, bf16[256,640]{1,0:T(8,128)(2,1)} %s.1), custom_call_target="tpu_custom_call" | custom-call | tf_op jit(solution)/shard_map/pallas_call | solution.py:266
  44.4 0.6 %add_rsqrt_fusion = (f32[2]{0:T(128)S(1)}, f32[2]{0:T(128)}, f32[2]{0:T(128)}) fusion(f32[4]{0:T(128)S(1)} %get-tuple-element.5), kind=kLoop, calls=%fused_computation.1 | loop fusion | flops 2 | bytes 40 | tf_op jit(solution)/shard_map/rsqrt | solution.py:292
  45.0 1.3 %multiply_convert_fusion = bf16[2,256,1024]{2,1,0:T(8,128)(2,1)} fusion(f32[2,256,1024]{2,1,0:T(8,128)S(1)} %get-tuple-element.6, f32[2]{0:T(128)S(1)} %get-tuple-element.7), kind=kLoop, calls=%fused_computation | loop fusion | flops 1048576 | bytes 3145736 | tf_op jit(solution)/shard_map/convert_element_type | solution.py:293

commit v3 on v2

--- a/solution.py
+++ b/solution.py
@@ -52,9 +52,9 @@
     return out
 
 
-def body(domains, groups, chunk, pat_hbm, x, h, s, out, facts,
+def body(domains, groups, inner, chunk, pat_hbm, x, h, s, out, facts,
          pat, ext, oth, hp, sp, pick, hext, img, acc, slots, nslots,
-         lsem, nb_send, nb_recv, tr_send, tr_recv, st_send, st_recv, nm_send, nm_recv):
+         lsem, nb_send, nb_recv, tr_send, tr_recv, st_send, st_recv, nm_send, nm_recv, ready):
     own, rows, width = x.shape
     atoms_dev, nslot = pat.shape
     block = rows // atoms_dev
@@ -76,13 +76,17 @@
 
     barrier = pltpu.get_barrier_semaphore()
 
-    def greet(k, carry):
-        pl.semaphore_signal(barrier, inc=1, device_id={"space": lax.rem(me + k, domains)})
-        return carry
-    lax.fori_loop(1, domains, greet, 0)
+    outer = domains // inner
+    spot_in, spot_out = lax.rem(me, inner), me // inner
+    first_in = me - spot_in
+    friends = [right, left]
+    friends += [first_in + lax.rem(spot_in + k, inner) for k in range(1, inner)]
+    friends += [spot_in + inner * lax.rem(spot_out + k, outer) for k in range(1, outer)]
+    for friend in friends:
+        pl.semaphore_signal(barrier, inc=1, device_id={"space": friend})
     for k in range(1, groups):
         pl.semaphore_signal(barrier, inc=1, device_id={"trial": lax.rem(mt + k, groups)})
-    pl.semaphore_wait(barrier, domains - 1 + groups - 1)
+    pl.semaphore_wait(barrier, len(friends) + groups - 1)
 
     def neighbour_copy(side, c):
         cols = pl.ds(pl.multiple_of(c * chunk, chunk), chunk)
@@ -105,6 +109,13 @@
     for c in range(chunks):
         for copy in arrivals(c):
             copy.start()
+
+    vouched = [spot_in + inner * lax.rem(spot_out + k, outer) for k in range(1, outer)]
+    for friend in vouched:
+        pl.semaphore_signal(ready, inc=1, device_id={"space": friend})
+    pl.semaphore_wait(ready, outer - 1)
+    peers = [lax.rem(spot_out + ko, outer) * inner + lax.rem(spot_in + ki, inner)
+             for ko in list(range(1, outer)) + [0] for ki in range(inner) if ko or ki]
 
     acc[...] = jnp.zeros_like(acc)
     loads[1].wait()
@@ -178,36 +189,25 @@
             message = jnp.where(spot == (g % 16) * 8, jnp.broadcast_to(ends, (8, 128)), message)
         slots[me, line:line + 1] = jnp.sum(message, axis=0, keepdims=True)
 
+    unsent = []
+
     def share(buffer, send, recv):
-        def copy(k):
+        def copy(k, place, to):
             return pltpu.make_async_remote_copy(
-                src_ref=buffer.at[me], dst_ref=buffer.at[me],
-                send_sem=send.at[k], recv_sem=recv.at[me],
-                device_id={"space": lax.rem(me + k, domains)})
-
-        def go(k, carry):
-            copy(k).start()
-            return carry
-        lax.fori_loop(1, domains, go, 0)
-
-        def come(k, carry):
-            peer = lax.rem(me + k, domains)
-            pltpu.make_async_remote_copy(
-                src_ref=buffer.at[peer], dst_ref=buffer.at[peer],
-                send_sem=send.at[k], recv_sem=recv.at[peer],
-                device_id={"space": peer}).wait_recv()
-            return carry
-        lax.fori_loop(1, domains, come, 0)
-
-        def left_here(k, carry):
-            copy(k).wait_send()
-            return carry
-        return lambda: lax.fori_loop(1, domains, left_here, 0)
-
-    end_stats = share(slots, st_send, st_recv)
-    total = slots[0]
-    for d in range(1, domains):
-        total = total + slots[d]
+                src_ref=buffer.at[place], dst_ref=buffer.at[place],
+                send_sem=send.at[k], recv_sem=recv.at[place], device_id={"space": to})
+        for k, peer in enumerate(peers):
+            away = copy(k, me, peer)
+            away.start()
+            unsent.append(away)
+        for k, peer in enumerate(peers):
+            copy(k, peer, peer).wait_recv()
+        result = buffer[0]
+        for d in range(1, domains):
+            result = result + buffer[d]
+        return result
+
+    total = share(slots, st_send, st_recv)
     value = {}
     for i, name in enumerate(pairs):
         value[name] = jnp.broadcast_to(total[i // 128:i // 128 + 1, i % 128:i % 128 + 1], (8, 128))
@@ -240,20 +240,21 @@
                 sums[k] = sums[k] + (p[:8] + p[8:])
         return tuple(sums)
     sums = lax.fori_loop(0, rows // 16, on_normal, (zero,) * own)
+    lane = lax.broadcasted_iota(jnp.int32, (1, 128), 1)
+    packed = jnp.zeros((1, 128), F32)
     for k in range(own):
-        nslots[me, k:k + 1] = jnp.sum(sums[k], axis=0, keepdims=True)
-    end_norms = share(nslots, nm_send, nm_recv)
-    norm = nslots[0]
-    for d in range(1, domains):
-        norm = norm + nslots[d]
-    norm = jnp.sum(norm, axis=1, keepdims=True) / float(domains * rows * width)
+        line = jnp.sum(jnp.sum(sums[k], axis=0, keepdims=True), axis=1, keepdims=True)
+        packed = jnp.where(lane == k, jnp.broadcast_to(line, (1, 128)), packed)
+    nslots[me] = packed
+    norm = share(nslots, nm_send, nm_recv)
+    norm = norm / float(domains * rows * width)
     for k in range(own):
-        facts[own + k] = norm[k, 0]
+        facts[own + k] = norm[0, k]
     for c in range(chunks):
         for copy in arrivals(c):
             copy.wait_send()
-    end_stats()
-    end_norms()
+    for copy in unsent:
+        copy.wait_send()
 
 
 def on_device(domains, groups, trial_x, h_panel, s_panel, pattern):
@@ -263,8 +264,10 @@
     chunks = width // chunk
     stats = -(-len(stat_pairs(own, own * groups)) // 8) * 8
     dma = pltpu.SemaphoreType.DMA
+    inner = max(d for d in range(1, domains + 1) if domains % d == 0 and d * d <= domains)
+    outer = domains // inner
     normal, facts = pl.pallas_call(
-        functools.partial(body, domains, groups, chunk),
+        functools.partial(body, domains, groups, inner, chunk),
         out_shape=(jax.ShapeDtypeStruct(trial_x.shape, F32), jax.ShapeDtypeStruct((2 * own,), F32)),
         in_specs=[pl.BlockSpec(memory_space=pltpu.HBM)] * 4,
         out_specs=(pl.BlockSpec(memory_space=pltpu.VMEM), pl.BlockSpec(memory_space=pltpu.SMEM)),
@@ -279,11 +282,12 @@
             pltpu.VMEM((own, 2 * rows, width), F32),
             pltpu.VMEM((stats, 8, 128), F32),
             pltpu.VMEM((domains, -(-stats // 128), 128), F32),
-            pltpu.VMEM((domains, own, 128), F32),
+            pltpu.VMEM((domains, 1, 128), F32),
             dma((4,)),
             dma((2, chunks)), dma((2, chunks)),
             dma((groups - 1, chunks)), dma((groups - 1, chunks)),
             dma((domains,)), dma((domains,)), dma((domains,)), dma((domains,)),
+            pltpu.SemaphoreType.REGULAR,
         ],
         compiler_params=pltpu.CompilerParams(
             collective_id=0, has_side_effects=True, vmem_limit_bytes=40 * 1024 * 1024),

time: 46.4 us -> 44.7 us (0.963)
  Pallas kernels: 43.7 us -> 42.1 us
    pallas_call x1, Pallas kernels: 43.7 us -> 42.1 us  [on_device(): pl.pallas_call(functools.partial(body, domains, groups, inner, chunk), ou...]
where the time goes in v3:
time: 44.7 us; the launch traced here: 44.6 us
  Pallas kernels  42.1 us (94%)
  other arithmetic  1.85 us (4%)
  between operations  0.64 us (1%)
    pallas_call x1, Pallas kernels, on_device(): pl.pallas_call(functools.partial(body, domains, groups, inner, chunk), ou...  42.1 us
    convert_element_type x1, other arithmetic, on_device(): return (theta, scaled.astype(BF16), mean_sq)  1.27 us

profile of v3, /device:TPU:0, one launch (start us, length us, event | category | flops | bytes accessed | tf_op | source)
XLA Modules:
  0.0 44.6 jit_solution(13523805986506093398)
XLA Ops:
  0.6 42.1 %shard_map.67 = (f32[2,256,1024]{2,1,0:T(8,128)S(1)}, f32[4]{0:T(128)S(1)}) custom-call(s32[4,10]{1,0:T(4,128)} %pat_hbm.1, bf16[2,256,1024]{2,1,0:T(8,128)(2,1)} %x.1, bf16[256,640]{1,0:T(8,128)(2,1)} %h.1, bf16[256,640]{1,0:T(8,128)(2,1)} %s.1), custom_call_target="tpu_custom_call" | custom-call | tf_op jit(solution)/shard_map/pallas_call | solution.py:269
  42.7 0.6 %add_rsqrt_fusion = (f32[2]{0:T(128)S(1)}, f32[2]{0:T(128)}, f32[2]{0:T(128)}) fusion(f32[4]{0:T(128)S(1)} %get-tuple-element.5), kind=kLoop, calls=%fused_computation.1 | loop fusion | flops 2 | bytes 40 | tf_op jit(solution)/shard_map/rsqrt | solution.py:296
  43.3 1.3 %multiply_convert_fusion = bf16[2,256,1024]{2,1,0:T(8,128)(2,1)} fusion(f32[2,256,1024]{2,1,0:T(8,128)S(1)} %get-tuple-element.6, f32[2]{0:T(128)S(1)} %get-tuple-element.7), kind=kLoop, calls=%fused_computation | loop fusion | flops 1048576 | bytes 3145736 | tf_op jit(solution)/shard_map/convert_element_type | solution.py:297

commit v4 on v3

--- a/solution.py
+++ b/solution.py
@@ -189,25 +189,27 @@
             message = jnp.where(spot == (g % 16) * 8, jnp.broadcast_to(ends, (8, 128)), message)
         slots[me, line:line + 1] = jnp.sum(message, axis=0, keepdims=True)
 
-    unsent = []
-
-    def share(buffer, send, recv):
-        def copy(k, place, to):
+    def share(buffer, send, recv, meanwhile):
+        def copy(place, to):
             return pltpu.make_async_remote_copy(
                 src_ref=buffer.at[place], dst_ref=buffer.at[place],
-                send_sem=send.at[k], recv_sem=recv.at[place], device_id={"space": to})
-        for k, peer in enumerate(peers):
-            away = copy(k, me, peer)
-            away.start()
-            unsent.append(away)
-        for k, peer in enumerate(peers):
-            copy(k, peer, peer).wait_recv()
+                send_sem=send, recv_sem=recv, device_id={"space": to})
+        for peer in peers:
+            copy(me, peer).start()
+        meanwhile()
+        every = copy(pl.ds(0, domains - 1), right)
+        every.wait_recv()
         result = buffer[0]
         for d in range(1, domains):
             result = result + buffer[d]
-        return result
-
-    total = share(slots, st_send, st_recv)
+        return result, every.wait_send
+
+    def bulk_gone():
+        for c in range(chunks):
+            for copy in arrivals(c):
+                copy.wait_send()
+
+    total, stats_gone = share(slots, st_send, st_recv, bulk_gone)
     value = {}
     for i, name in enumerate(pairs):
         value[name] = jnp.broadcast_to(total[i // 128:i // 128 + 1, i % 128:i % 128 + 1], (8, 128))
@@ -246,15 +248,11 @@
         line = jnp.sum(jnp.sum(sums[k], axis=0, keepdims=True), axis=1, keepdims=True)
         packed = jnp.where(lane == k, jnp.broadcast_to(line, (1, 128)), packed)
     nslots[me] = packed
-    norm = share(nslots, nm_send, nm_recv)
+    norm, norms_gone = share(nslots, nm_send, nm_recv, stats_gone)
     norm = norm / float(domains * rows * width)
     for k in range(own):
         facts[own + k] = norm[0, k]
-    for c in range(chunks):
-        for copy in arrivals(c):
-            copy.wait_send()
-    for copy in unsent:
-        copy.wait_send()
+    norms_gone()
 
 
 def on_device(domains, groups, trial_x, h_panel, s_panel, pattern):
@@ -286,7 +284,7 @@
             dma((4,)),
             dma((2, chunks)), dma((2, chunks)),
             dma((groups - 1, chunks)), dma((groups - 1, chunks)),
-            dma((domains,)), dma((domains,)), dma((domains,)), dma((domains,)),
+            dma, dma, dma, dma,
             pltpu.SemaphoreType.REGULAR,
         ],
         compiler_params=pltpu.CompilerParams(

time: 44.7 us -> 44.1 us (0.987)
  Pallas kernels: 42.1 us -> 41.5 us
    pallas_call x1, Pallas kernels: 42.1 us -> 41.5 us  [on_device(): pl.pallas_call(functools.partial(body, domains, groups, inner, chunk), ou...]
where the time goes in v4:
time: 44.1 us; the launch traced here: 44 us
  Pallas kernels  41.5 us (94%)
  other arithmetic  1.85 us (4%)
  between operations  0.64 us (1%)
    pallas_call x1, Pallas kernels, on_device(): pl.pallas_call(functools.partial(body, domains, groups, inner, chunk), ou...  41.5 us
    convert_element_type x1, other arithmetic, on_device(): return (theta, scaled.astype(BF16), mean_sq)  1.27 us

profile of v4, /device:TPU:0, one launch (start us, length us, event | category | flops | bytes accessed | tf_op | source)
XLA Modules:
  0.0 44.0 jit_solution(4010703178979683624)
XLA Ops:
  0.6 41.5 %shard_map.67 = (f32[2,256,1024]{2,1,0:T(8,128)S(1)}, f32[4]{0:T(128)S(1)}) custom-call(s32[4,10]{1,0:T(4,128)} %pat_hbm.1, bf16[2,256,1024]{2,1,0:T(8,128)(2,1)} %x.1, bf16[256,640]{1,0:T(8,128)(2,1)} %h.1, bf16[256,640]{1,0:T(8,128)(2,1)} %s.1), custom_call_target="tpu_custom_call" | custom-call | tf_op jit(solution)/shard_map/pallas_call | solution.py:267
  42.1 0.6 %add_rsqrt_fusion = (f32[2]{0:T(128)S(1)}, f32[2]{0:T(128)}, f32[2]{0:T(128)}) fusion(f32[4]{0:T(128)S(1)} %get-tuple-element.5), kind=kLoop, calls=%fused_computation.1 | loop fusion | flops 2 | bytes 40 | tf_op jit(solution)/shard_map/rsqrt | solution.py:294
  42.7 1.3 %multiply_convert_fusion = bf16[2,256,1024]{2,1,0:T(8,128)(2,1)} fusion(f32[2,256,1024]{2,1,0:T(8,128)S(1)} %get-tuple-element.6, f32[2]{0:T(128)S(1)} %get-tuple-element.7), kind=kLoop, calls=%fused_computation | loop fusion | flops 1048576 | bytes 3145736 | tf_op jit(solution)/shard_map/convert_element_type | solution.py:295

commit v5 on v4

--- a/solution.py
+++ b/solution.py
@@ -104,7 +104,7 @@
             device_id={"trial": lax.rem(mt + k, groups)})
 
     def arrivals(c):
-        return [neighbour_copy(0, c), neighbour_copy(1, c)] + [trial_copy(k, c) for k in range(1, groups)]
+        return [trial_copy(k, c) for k in range(1, groups)] + [neighbour_copy(0, c), neighbour_copy(1, c)]
 
     for c in range(chunks):
         for copy in arrivals(c):
@@ -258,7 +258,7 @@
 def on_device(domains, groups, trial_x, h_panel, s_panel, pattern):
     own, rows, width = trial_x.shape
     depth = h_panel.shape[1]
-    chunk = 256
+    chunk = 128
     chunks = width // chunk
     stats = -(-len(stat_pairs(own, own * groups)) // 8) * 8
     dma = pltpu.SemaphoreType.DMA

time: 44.1 us -> 44.1 us (level)
  no operation moved by 1% of the time
where the time goes in v5:
time: 44.1 us; the launch traced here: 43.9 us
  Pallas kernels  41.5 us (94%)
  other arithmetic  1.85 us (4%)
  between operations  0.64 us (1%)
    pallas_call x1, Pallas kernels, on_device(): pl.pallas_call(functools.partial(body, domains, groups, inner, chunk), ou...  41.5 us
    convert_element_type x1, other arithmetic, on_device(): return (theta, scaled.astype(BF16), mean_sq)  1.27 us

profile of v5, /device:TPU:0, one launch (start us, length us, event | category | flops | bytes accessed | tf_op | source)
XLA Modules:
  0.0 43.9 jit_solution(9475336236443425548)
XLA Ops:
  0.6 41.5 %shard_map.67 = (f32[2,256,1024]{2,1,0:T(8,128)S(1)}, f32[4]{0:T(128)S(1)}) custom-call(s32[4,10]{1,0:T(4,128)} %pat_hbm.1, bf16[2,256,1024]{2,1,0:T(8,128)(2,1)} %x.1, bf16[256,640]{1,0:T(8,128)(2,1)} %h.1, bf16[256,640]{1,0:T(8,128)(2,1)} %s.1), custom_call_target="tpu_custom_call" | custom-call | tf_op jit(solution)/shard_map/pallas_call | solution.py:267
  42.1 0.6 %add_rsqrt_fusion = (f32[2]{0:T(128)S(1)}, f32[2]{0:T(128)}, f32[2]{0:T(128)}) fusion(f32[4]{0:T(128)S(1)} %get-tuple-element.5), kind=kLoop, calls=%fused_computation.1 | loop fusion | flops 2 | bytes 40 | tf_op jit(solution)/shard_map/rsqrt | solution.py:294
  42.7 1.3 %multiply_convert_fusion = bf16[2,256,1024]{2,1,0:T(8,128)(2,1)} fusion(f32[2,256,1024]{2,1,0:T(8,128)S(1)} %get-tuple-element.6, f32[2]{0:T(128)S(1)} %get-tuple-element.7), kind=kLoop, calls=%fused_computation | loop fusion | flops 1048576 | bytes 3145736 | tf_op jit(solution)/shard_map/convert_element_type | solution.py:295
